TPU v7x, 256 devices: a whole 4x4x8 slice. The times are simulated.
256 devices in a mesh: table: 16 (over y_lo, x, core), tensor: 2 (over y_hi), dp: 8 (over z).
Axes of the slice: x: 4, y: 4 (y_hi: 2, y_lo: 2; y = y_hi * 2 + y_lo), z: 8, core: 2. Of those that a mesh axis runs over, the one named last changes fastest.
Arguments:
- lookup_ids: int32 [4096, 16, 16], P('dp', 'table'), may hold values from 0 to 4095
- bag_lengths: int32 [4096, 16], P('dp', 'table'), may hold values from 1 to 16
- feature_widths: int32 [16], replicated, may hold values from 32 to 256, as said below
- tables: bfloat16 [16, 4096, 256], P('table', None, 'tensor'), may hold values from -6 to 6
- w_in: bfloat16 [4096, 16384], P(None, ('table', 'tensor')), may hold values from -0.25 to 0.25
- w_out: bfloat16 [16384, 4096], P(('table', 'tensor')), may hold values from -0.1875 to 0.1875
- cotangent: bfloat16 [4096, 4096], P('dp', ('table', 'tensor')), may hold values from -6 to 6
Outputs:
- mixed_out: bfloat16 [4096, 4096], P('dp', ('table', 'tensor'))
- grad_in: float32 [4096, 16384], P('dp', ('table', 'tensor'))
- grad_out: float32 [16384, 4096], P(('table', 'tensor', 'dp'))
Inputs may be any that keep to these rules, and one draw needn't show every extreme that they name: `feature_widths`: multiples of 32; one feature has exactly 256, another exactly 32.
All inputs are finite; a program needn't handle non-finite values.
Results may differ from a plain program's by a relative error of at most 0.0056.
Values may be sent and summed in bfloat16 or wider, within the bound.
A program may use at most 128 MiB of HBM per device.

v0:
```python
import jax
import jax.numpy as jnp
from jax import lax
from jax.sharding import PartitionSpec as P


def silu_slope(preact):
    sigmoid_part = jax.nn.sigmoid(preact)
    return sigmoid_part * (1.0 + preact * (1.0 - sigmoid_part))


def pool_local(lookup, lengths, embedding):
    samples, bag_size = lookup.shape
    vocab, half_width = embedding.shape
    vocab_block = min(vocab, 512)
    in_bag = jnp.arange(bag_size)[None, :] < lengths[:, None]
    masked = jnp.where(in_bag, lookup, -1)

    def add_block(running, first_row):
        local_ids = first_row + jnp.arange(vocab_block)
        counts = jnp.sum(masked[:, :, None] == local_ids[None, None, :], axis=1).astype(
            jnp.bfloat16
        )
        table_rows = lax.dynamic_slice_in_dim(embedding, first_row, vocab_block, 0)
        return (running + jnp.dot(counts, table_rows, preferred_element_type=jnp.float32), None)

    starts = jnp.arange(vocab // vocab_block) * vocab_block
    summed, unused = lax.scan(add_block, jnp.zeros((samples, half_width), jnp.float32), starts)
    return summed / lengths[:, None].astype(jnp.float32)


def shards(lookup_ids, bag_lengths, feature_widths, tables, w_in, w_out, cotangent):
    embedding = tables[0]
    half_width = embedding.shape[1]
    summed = pool_local(lookup_ids[:, 0, :], bag_lengths[:, 0], embedding)
    own_width = lax.dynamic_index_in_dim(feature_widths, lax.axis_index("table"), 0, keepdims=False)
    positions = lax.axis_index("tensor") * half_width + jnp.arange(half_width)
    pooled = jnp.where(positions[None, :] < own_width, summed, jnp.zeros_like(summed)).astype(
        jnp.bfloat16
    )
    features = lax.all_gather(pooled, ("table", "tensor"), axis=1, tiled=True)
    preact = jnp.dot(features, w_in, preferred_element_type=jnp.float32)
    hidden = jax.nn.silu(preact).astype(jnp.bfloat16)
    partial_out = jnp.dot(hidden, w_out, preferred_element_type=jnp.float32)
    reduced = lax.psum_scatter(partial_out, ("table", "tensor"), scatter_dimension=1, tiled=True)
    mixed_out = reduced.astype(jnp.bfloat16)
    whole_grad = lax.all_gather(cotangent, ("table", "tensor"), axis=1, tiled=True)
    contract_rows = (((0,), (0,)), ((), ()))
    contract_cols = (((1,), (1,)), ((), ()))
    grad_hidden = lax.dot_general(
        whole_grad, w_out, contract_cols, preferred_element_type=jnp.float32
    )
    grad_preact = (grad_hidden * silu_slope(preact)).astype(jnp.bfloat16)
    term_in = lax.dot_general(
        features, grad_preact, contract_rows, preferred_element_type=jnp.float32
    )
    term_out = lax.dot_general(
        hidden, whole_grad, contract_rows, preferred_element_type=jnp.float32
    )
    grad_in, grad_out = (
        lax.psum_scatter(term_in, "dp", scatter_dimension=0, tiled=True),
        lax.psum_scatter(term_out, "dp", scatter_dimension=0, tiled=True),
    )
    return (mixed_out, grad_in, grad_out)


def solution(mesh):
    return jax.shard_map(
        shards,
        mesh=mesh,
        in_specs=(
            P("dp", "table", None),
            P("dp", "table"),
            P(),
            P("table", None, "tensor"),
            P(None, ("table", "tensor")),
            P(("table", "tensor"), None),
            P("dp", ("table", "tensor")),
        ),
        out_specs=(
            P("dp", ("table", "tensor")),
            P("dp", ("table", "tensor")),
            P(("table", "tensor", "dp"), None),
        ),
        check_vma=False,
    )
```

profile of v0, /device:TPU:1, one launch (start us, length us, event | category | flops | bytes accessed | tf_op | source)
XLA Modules:
  0.0 646.2 jit_solution(7221660511315152307)
XLA Ops:
  7.9 0.9 copy.11
  8.8 0.8 bitcast_select_fusion
  9.6 64.7 %while.11 = (s32[]{:T(128)}, f32[512,128]{1,0:T(8,128)S(1)}, s32[512,16]{1,0:T(8,128)S(1)}, s32[8]{0:T(128)S(1)}, bf16[4096,128]{1,0:T(8,128)(2,1)}, /*index=5*/s32[]{:T(128)}, s32[]{:T(128)}, s32[]{:T(128)}) while((s32[]{:T(128)}, f32[512,128]{1,0:T(8,128)S(1)}, s32[512,16]{1,0:T(8,128)S(1)}, s32[8]{0:T(128)S(1)}, ...), condition=%wide.region_2.3_spmd.clone, body=%wide.region_0.2_spmd.clone.sunk | while | flops 79823368 | bytes 2789533 | solution.py:28
  12.8 3.6 convert_reduce_fusion.2
  16.5 1.2 convolution_add_fusion.2
  20.9 3.6 convert_reduce_fusion.2
  24.6 1.2 convolution_add_fusion.2
  29.0 3.6 convert_reduce_fusion.2
  32.7 1.2 convolution_add_fusion.2
  37.1 3.6 convert_reduce_fusion.2
  40.7 1.2 convolution_add_fusion.2
  45.2 3.6 convert_reduce_fusion.2
  48.8 1.2 convolution_add_fusion.2
  53.3 3.6 convert_reduce_fusion.2
  56.9 1.2 convolution_add_fusion.2
  61.4 3.6 convert_reduce_fusion.2
  65.0 1.2 convolution_add_fusion.2
  69.5 3.6 convert_reduce_fusion.2
  73.1 1.2 convolution_add_fusion.2
  75.6 0.8 select_convert_fusion
  76.5 0.7 all-gather.5.cloned.1.call-update
  77.2 89.7 %all-gather.3.cloned.1.call-done = bf16[512,4096]{1,0:T(8,128)(2,1)} async-done(((bf16[512,128]{1,0:T(8,128)(2,1)}), bf16[512,4096]{1,0:T(8,128)(2,1)}) %all-gather.3.cloned.1.call-update) | async-done | bytes 4194320 | tf_op jit(solution)/shard_map/all_gather | solution.py:41
  166.9 5.9 fusion.6
  172.8 5.6 fusion.5
  178.5 74.9 %all-gather.5.cloned.1.call-done = bf16[512,4096]{1,0:T(8,128)(2,1)} async-done(((bf16[512,128]{1,0:T(8,128)(2,1)}), bf16[512,4096]{1,0:T(8,128)(2,1)}) %all-gather.5.cloned.1.call-update) | async-done | bytes 4194320 | tf_op jit(solution)/shard_map/all_gather | solution.py:47
  253.4 6.1 fusion.3
  259.6 5.7 fusion.7
  265.3 7.9 %fusion.4 = f32[512,4096]{1,0:T(8,128)} fusion(bf16[512,4096]{1,0:T(8,128)(2,1)} %all-gather.5.cloned.1.call-done, f32[512,512]{1,0:T(8,128)S(1)} %fusion.6), kind=kOutput, calls=%fused_computation.15 | convolution fusion | flops 2148794368 | bytes 13631488 | tf_op jit(solution)/shard_map/dot_general | solution.py:57
  273.2 170.3 %reduce-scatter.4.cloned.1.call-done = f32[512,128]{1,0:T(8,128)} async-done(((f32[512,4096]{1,0:T(8,128)}), f32[512,128]{1,0:T(8,128)}) %reduce-scatter.4.cloned.1.call-update) | async-done | bytes 262160 | tf_op jit(solution)/shard_map/reduce_scatter | solution.py:45
  443.6 1.6 convert_element_type.24
  445.2 97.9 %reduce-scatter.6.cloned.1.call-done = f32[512,512]{1,0:T(8,128)} async-done(((f32[4096,512]{1,0:T(8,128)}), f32[512,512]{1,0:T(8,128)}) %reduce-scatter.6.cloned.1.call-update) | async-done | bytes 1048592 | tf_op jit(solution)/shard_map/reduce_scatter | solution.py:61
  543.1 96.6 %reduce-scatter.8.cloned.1.call-done = f32[64,4096]{1,0:T(8,128)} async-done(((f32[512,4096]{1,0:T(8,128)}), f32[64,4096]{1,0:T(8,128)}) %reduce-scatter.8.cloned.1.call-update) | async-done | bytes 1048592 | tf_op jit(solution)/shard_map/reduce_scatter | solution.py:62
  (36 shorter events, 12.1 us)
Async XLA Ops:
  7.2 159.7 %all-gather.3.cloned.1.call-start = ((), (), s32[]{:S(2)}) async-start(), calls=%async_computation.3 | async-start | bytes 4325376 | tf_op jit(solution)/shard_map/all_gather | solution.py:41
  9.6 64.7 %copy-start.2 = (s32[16]{0:T(128)S(1)}, s32[16]{0:T(128)}, u32[]{:S(2)}) copy-start(s32[16]{0:T(128)} %param.11) | copy-start | bytes 196
  76.4 177.0 %all-gather.5.cloned.1.call-start = ((), (), s32[]{:S(2)}) async-start(), calls=%async_computation.5 | async-start | bytes 4325376 | tf_op jit(solution)/shard_map/all_gather | solution.py:47
  77.2 366.4 %reduce-scatter.4.cloned.1.call-start = ((), (), s32[]{:S(2)}) async-start(), calls=%async_computation.4 | async-start | bytes 8650752 | tf_op jit(solution)/shard_map/reduce_scatter | solution.py:45
  166.9 5.9 copy-start.1
  178.5 364.6 %reduce-scatter.6.cloned.1.call-start = ((), (), s32[]{:S(2)}) async-start(), calls=%async_computation.6 | async-start | bytes 9437184 | tf_op jit(solution)/shard_map/reduce_scatter | solution.py:61
  253.4 6.1 copy-start
  265.3 374.5 %reduce-scatter.8.cloned.1.call-start = ((), (), s32[]{:S(2)}) async-start(), calls=%async_computation.7 | async-start | bytes 9437184 | tf_op jit(solution)/shard_map/reduce_scatter | solution.py:62
Sparse Core Ops, SparseCore 0:
  76.6 90.2 all-gather.2
  168.6 84.7 all-gather.4
  256.0 187.5 reduce-scatter.3
  446.5 96.5 reduce-scatter.5
  546.1 93.5 reduce-scatter.7
where the time goes:
time: 647 us; the launch traced here: 646 us
  waiting for transfers between devices  530 us (82%)
  matrix products  41.2 us (6%)
  other arithmetic  38.8 us (6%)
  loops' own time  15.9 us (2%)
  between operations  13.9 us (2%)
    reduce_scatter x1, waiting for transfers between devices, shards(): lax.psum_scatter(partial_out, ('table', 'tensor'), scatter_dimension=1, t...  170 us
    reduce_scatter x1, waiting for transfers between devices, shards(): lax.psum_scatter(term_in, 'dp', scatter_dimension=0, tiled=True)  97.9 us
    reduce_scatter x1, waiting for transfers between devices, shards(): lax.psum_scatter(term_out, 'dp', scatter_dimension=0, tiled=True)  96.6 us
    all_gather x1, waiting for transfers between devices, shards(): features = lax.all_gather(pooled, ('table', 'tensor'), axis=1, tiled=True)  89.7 us
    all_gather x1, waiting for transfers between devices, shards(): lax.all_gather(cotangent, ('table', 'tensor'), axis=1, tiled=True)  74.9 us
    reduce_sum x8, other arithmetic, add_block(): jnp.sum(masked[:, :, None] == local_ids[None, None, :], axis=1)  29 us
    another operation x1, loops' own time, pool_local(): lax.scan(add_block, jnp.zeros((samples, half_width), jnp.float32), starts)  15.9 us
  transfers between devices with their start and end apart: 5, of which 5 were waited for; matrix products, arithmetic and copies ran while one was open for 5% of the time, Pallas kernels for 0%

commit v1 on v0

--- a/solution.py
+++ b/solution.py
@@ -1,7 +1,21 @@
+import functools
 import jax
 import jax.numpy as jnp
 from jax import lax
 from jax.sharding import PartitionSpec as P
+from jax.lax import all_to_all, axis_size
+
+
+def fit_pipes(frame, in_dim):
+    return jnp.concatenate(
+        all_to_all(
+            jnp.stack(axis_size(("table", "tensor")) * [frame], 0), ("table", "tensor"), 0, 0
+        ),
+        in_dim,
+    )
+
+
+weights_follow = functools.partial(fit_pipes, in_dim=1)
 
 
 def silu_slope(preact):
@@ -38,7 +52,7 @@
     pooled = jnp.where(positions[None, :] < own_width, summed, jnp.zeros_like(summed)).astype(
         jnp.bfloat16
     )
-    features = lax.all_gather(pooled, ("table", "tensor"), axis=1, tiled=True)
+    features = weights_follow(pooled)
     preact = jnp.dot(features, w_in, preferred_element_type=jnp.float32)
     hidden = jax.nn.silu(preact).astype(jnp.bfloat16)
     partial_out = jnp.dot(hidden, w_out, preferred_element_type=jnp.float32)

time: 647 us -> 541 us (0.84)
  waiting for transfers between devices: 530 us -> 366 us
  blocking collectives: 0 us -> 61.2 us
    all_gather x1 -> x0, waiting for transfers between devices: 89.7 us -> none  [shards(): features = lax.all_gather(pooled, ('table', 'tensor'), axis=1, tiled=True)]
    all_gather x1, waiting for transfers between devices: 74.9 us -> 0.02 us  [shards(): lax.all_gather(cotangent, ('table', 'tensor'), axis=1, tiled=True)]
    all_to_all x0 -> x1, blocking collectives: none -> 61.2 us  [fit_pipes(): all_to_all(jnp.stack(axis_size(('table', 'tensor')) * [frame], 0), ('tabl...]
  transfers between devices with their start and end apart: 5 -> 4, of which waited for: 5 -> 3; matrix products, arithmetic and copies ran while one was open for 5% -> 15% of each run, Pallas kernels for 0% -> 0%
where the time goes in v1:
time: 541 us
  waiting for transfers between devices  366 us (68%)
  blocking collectives  61.2 us (11%)
  matrix products  37.6 us (7%)
  other arithmetic  37.4 us (7%)
  loops' own time  15.9 us (3%)
  between operations  13.9 us (3%)
  local copies, waits for them, and re-layouts  8.72 us (2%)
    reduce_scatter x1, waiting for transfers between devices, shards(): lax.psum_scatter(partial_out, ('table', 'tensor'), scatter_dimension=1, t...  170 us
    reduce_scatter x1, waiting for transfers between devices, shards(): lax.psum_scatter(term_in, 'dp', scatter_dimension=0, tiled=True)  98.2 us
    reduce_scatter x1, waiting for transfers between devices, shards(): lax.psum_scatter(term_out, 'dp', scatter_dimension=0, tiled=True)  96.6 us
    all_to_all x1, blocking collectives, fit_pipes(): all_to_all(jnp.stack(axis_size(('table', 'tensor')) * [frame], 0), ('tabl...  61.2 us
    reduce_sum x8, other arithmetic, add_block(): jnp.sum(masked[:, :, None] == local_ids[None, None, :], axis=1)  29 us
    another operation x1, loops' own time, pool_local(): lax.scan(add_block, jnp.zeros((samples, half_width), jnp.float32), starts)  15.9 us
  transfers between devices with their start and end apart: 4, of which 3 were waited for; matrix products, arithmetic and copies ran while one was open for 15% of the time, Pallas kernels for 0%

profile of v1, /device:TPU:1, one launch (start us, length us, event | category | flops | bytes accessed | tf_op | source)
XLA Modules:
  0.0 540.7 jit_solution(6568333351670892574)
XLA Ops:
  7.2 0.7 all-gather.2.cloned.1.call-update
  8.0 0.9 copy.13
  8.9 0.8 bitcast_select_fusion
  9.7 64.7 %while.11 = (s32[]{:T(128)}, f32[512,128]{1,0:T(8,128)S(1)}, s32[512,16]{1,0:T(8,128)S(1)}, s32[8]{0:T(128)S(1)}, bf16[4096,128]{1,0:T(8,128)(2,1)}, /*index=5*/s32[]{:T(128)}, s32[]{:T(128)}, s32[]{:T(128)}) while((s32[]{:T(128)}, f32[512,128]{1,0:T(8,128)S(1)}, s32[512,16]{1,0:T(8,128)S(1)}, s32[8]{0:T(128)S(1)}, ...), condition=%wide.region_2.3_spmd.clone, body=%wide.region_0.2_spmd.clone.sunk | while | flops 79823368 | bytes 2789533 | solution.py:42
  12.9 3.6 convert_reduce_fusion.2
  16.5 1.2 convolution_add_fusion.2
  21.0 3.6 convert_reduce_fusion.2
  24.6 1.2 convolution_add_fusion.2
  29.1 3.6 convert_reduce_fusion.2
  32.7 1.2 convolution_add_fusion.2
  37.2 3.6 convert_reduce_fusion.2
  40.8 1.2 convolution_add_fusion.2
  45.3 3.6 convert_reduce_fusion.2
  48.9 1.2 convolution_add_fusion.2
  52.7 0.7 iota_add_fusion.2
  53.4 3.6 convert_reduce_fusion.2
  57.0 1.2 convolution_add_fusion.2
  61.4 3.6 convert_reduce_fusion.2
  65.1 1.2 convolution_add_fusion.2
  69.5 3.6 convert_reduce_fusion.2
  73.2 1.2 convolution_add_fusion.2
  76.5 61.2 %all_to_all.5 = bf16[32,512,128]{1,2,0:T(8,128)(2,1)S(1)} all-to-all(bf16[32,512,128]{1,2,0:T(8,128)(2,1)S(1)} %stack.2), channel_id=1, replica_groups=mesh['table'=16,'tensor'=2,'dp'=8] {'table','tensor'}, dimensions={0} | all-to-all | bytes 8388608 | tf_op jit(solution)/shard_map/all_to_all | solution.py:11
  137.7 2.0 copy-done
  139.6 2.3 fusion.6
  142.0 5.6 %fusion.5 = f32[512,4096]{1,0:T(8,128)} fusion(bf16[512,4096]{1,0:T(8,128)(2,1)S(1)} %copy-done.3, f32[512,512]{1,0:T(8,128)S(1)} %fusion.6), kind=kOutput, calls=%fused_computation.16 | convolution fusion | flops 2148794368 | bytes 13631488 | tf_op jit(solution)/shard_map/dot_general | solution.py:58
  147.7 6.1 %fusion.3 = bf16[512,512]{1,0:T(8,128)(2,1)S(1)} fusion(bf16[512,4096]{1,0:T(8,128)(2,1)} %all-gather.2.cloned.1.call-done, bf16[512,4096]{1,0:T(8,128)(2,1)} %param.14, f32[512,512]{1,0:T(8,128)S(1)} %fusion.6), kind=kOutput, calls=%fused_computation.7 | convolution fusion | flops 2149842944 | bytes 9961472 | tf_op jit(solution)/shard_map/dot_general | solution.py:64
  153.9 5.7 %fusion.7 = f32[4096,512]{1,0:T(8,128)} fusion(bf16[512,4096]{0,1:T(8,128)(2,1)S(1)} %bitcast.21, bf16[512,512]{1,0:T(8,128)(2,1)S(1)} %fusion.3), kind=kOutput, calls=%fused_computation.18 | convolution fusion | flops 2147483648 | bytes 13107200 | tf_op jit(solution)/shard_map/dot_general | solution.py:68
  159.6 7.9 %fusion.4 = f32[512,4096]{1,0:T(8,128)} fusion(bf16[512,4096]{1,0:T(8,128)(2,1)} %all-gather.2.cloned.1.call-done, f32[512,512]{1,0:T(8,128)S(1)} %fusion.6), kind=kOutput, calls=%fused_computation.15 | convolution fusion | flops 2148794368 | bytes 13631488 | tf_op jit(solution)/shard_map/dot_general | solution.py:71
  167.5 170.3 %reduce-scatter.4.cloned.1.call-done = f32[512,128]{1,0:T(8,128)} async-done(((f32[512,4096]{1,0:T(8,128)}), f32[512,128]{1,0:T(8,128)}) %reduce-scatter.4.cloned.1.call-update) | async-done | bytes 262160 | tf_op jit(solution)/shard_map/reduce_scatter | solution.py:59
  337.8 1.6 convert_element_type.24
  339.4 98.2 %reduce-scatter.6.cloned.1.call-done = f32[512,512]{1,0:T(8,128)} async-done(((f32[4096,512]{1,0:T(8,128)}), f32[512,512]{1,0:T(8,128)}) %reduce-scatter.6.cloned.1.call-update) | async-done | bytes 1048592 | tf_op jit(solution)/shard_map/reduce_scatter | solution.py:75
  437.6 96.6 %reduce-scatter.8.cloned.1.call-done = f32[64,4096]{1,0:T(8,128)} async-done(((f32[512,4096]{1,0:T(8,128)}), f32[64,4096]{1,0:T(8,128)}) %reduce-scatter.8.cloned.1.call-update) | async-done | bytes 1048592 | tf_op jit(solution)/shard_map/reduce_scatter | solution.py:76
  (42 shorter events, 11.4 us)
Async XLA Ops:
  7.2 140.6 %all-gather.2.cloned.1.call-start = ((), (), s32[]{:S(2)}) async-start(), calls=%async_computation.5 | async-start | bytes 4325376 | tf_op jit(solution)/shard_map/all_gather | solution.py:61
  7.9 329.9 %reduce-scatter.4.cloned.1.call-start = ((), (), s32[]{:S(2)}) async-start(), calls=%async_computation.4 | async-start | bytes 8650752 | tf_op jit(solution)/shard_map/reduce_scatter | solution.py:59
  9.7 64.7 %copy-start.4 = (s32[512,1]{0,1:T(1,128)S(1)}, s32[512,1]{0,1:T(1,128)}, u32[]{:S(2)}) copy-start(s32[512,1]{0,1:T(1,128)} %param.10) | copy-start | bytes 6148
  9.7 64.8 %copy-start.5 = (s32[16]{0:T(128)S(1)}, s32[16]{0:T(128)}, u32[]{:S(2)}) copy-start(s32[16]{0:T(128)} %param.11) | copy-start | bytes 196
  76.4 63.2 %copy-start.2 = (bf16[4096,512]{1,0:T(8,128)(2,1)S(1)}, bf16[4096,512]{1,0:T(8,128)(2,1)}, u32[]{:S(2)}) copy-start(bf16[4096,512]{1,0:T(8,128)(2,1)} %param.13) | copy-start | bytes 12582916
  137.7 2.0 copy-start
  139.6 2.4 copy-start.3
  147.6 289.9 %reduce-scatter.6.cloned.1.call-start = ((), (), s32[]{:S(2)}) async-start(), calls=%async_computation.6 | async-start | bytes 9437184 | tf_op jit(solution)/shard_map/reduce_scatter | solution.py:75
  147.7 6.1 %copy-start.1 = (bf16[32,512,128]{1,2,0:T(8,128)(2,1)S(1)}, bf16[32,512,128]{1,2,0:T(8,128)(2,1)}, u32[]{:S(2)}) copy-start(bf16[32,512,128]{1,2,0:T(8,128)(2,1)} %copy-done) | copy-start | bytes 12582916
  159.6 374.6 %reduce-scatter.8.cloned.1.call-start = ((), (), s32[]{:S(2)}) async-start(), calls=%async_computation.7 | async-start | bytes 9437184 | tf_op jit(solution)/shard_map/reduce_scatter | solution.py:76
Sparse Core Ops, SparseCore 0:
  9.7 119.7 all-gather.1
  147.8 190.0 reduce-scatter.3
  341.0 96.5 reduce-scatter.5
  440.6 93.5 reduce-scatter.7
